TPU v7x, 32 devices: a whole 2x2x4 slice. The times are simulated.
32 devices in a mesh: groups: 2 (over y), seq: 4 (over z), head: 2 (over x), rep: 2 (over core).
Axes of the slice: x: 2, y: 2, z: 4, core: 2. Of those that a mesh axis runs over, the one named last changes fastest.
Arguments:
- book_tokens: bfloat16 [16384, 1024], P(('groups', 'seq', 'rep')), parts along dimension 0, may hold values from -6 to 6
- norm_gain: float32 [1024], replicated, may hold values from 0.1 to 1.9
- query_weight: bfloat16 [1024, 1024], P(None, 'head'), may hold values from -0.1875 to 0.1875
- key_weight: bfloat16 [1024, 1024], P(None, 'head'), may hold values from -0.1875 to 0.1875
- value_weight: bfloat16 [1024, 1024], P(None, 'head'), may hold values from -0.1875 to 0.1875
- proj_weight: bfloat16 [1024, 4096], P(None, 'head'), may hold values from -0.75 to 0.75
- dual_gains: float32 [4, 1024], P(None, 'head'), may hold values from 0.1 to 1.9
- out_weight: bfloat16 [1024, 1024], P(None, 'head'), may hold values from -1.5 to 1.5
- span_bounds: int32 [128, 2], P('groups'), parts along dimension 0, may hold values from 0 to 8192, as said below
Outputs:
- attended: bfloat16 [16384, 1024], P(('groups', 'seq', 'rep'), 'head'), parts along dimension 0
- pooled: float32 [128, 1024], P(('groups', 'seq', 'rep'), 'head'), parts along dimension 0
There are 2 independent parts, one for each index of `groups`. A program takes and returns all parts, laid end to end along the dimension named above; an argument that names none is the same for every part. Nothing has to cross between parts.
Inputs may be any that keep to these rules, and one draw needn't show every extreme that they name: `span_bounds`: each span lies inside the book and holds 1 to 512 tokens; spans may intersect and come in any order; the longest holds exactly 512 tokens.
All inputs are finite; a program needn't handle non-finite values.
Results may differ from a plain program's by a relative error of at most 0.023.
Values may be sent and summed in bfloat16 or wider, within the bound.
No kernel may reach another device: no remote copies, remote signals or barrier semaphores. Data moves between devices by JAX's collectives and lax.ppermute only.
A program may use at most 64 MiB of HBM per device.

v0:
```python
import jax
import jax.numpy as jnp
from jax import lax
from jax.sharding import PartitionSpec as P

DH = 64
R = 256
SEG = 128
softcap = 5.0
epsilon = 1e-05


def with_halo(cells, sides, width):
    for axis, dim in sides:
        count = lax.axis_size(axis)
        ends = count - 1
        head = lax.slice_in_dim(cells, 0, width, axis=dim)
        tail = lax.slice_in_dim(cells, cells.shape[dim] - width, cells.shape[dim], axis=dim)
        cells = jnp.concatenate(
            [
                lax.ppermute(tail, axis, [(i, (i + 1) % count) for i in range(ends)]),
                cells,
                lax.ppermute(head, axis, [((i + 1) % count, i) for i in range(ends)]),
            ],
            axis=dim,
        )
    return cells


def normalize(values, gain_row):
    centre = jnp.mean(values, axis=-1, keepdims=True)
    spread = jnp.mean(jnp.square(values - centre), axis=-1, keepdims=True)
    return (values - centre) * lax.rsqrt(spread + epsilon) * gain_row


def capped(values):
    return softcap * jnp.tanh(values / softcap)


def finish(total_numer, gain_rows):
    land_keys = normalize(total_numer[:, :, :DH], gain_rows[2][:, None, :])
    land_values = normalize(total_numer[:, :, DH:], gain_rows[3][:, None, :])
    return jnp.concatenate([land_keys, land_values], axis=-1).astype(jnp.bfloat16)


def per_device(
    book_tokens,
    norm_gain,
    query_weight,
    key_weight,
    value_weight,
    proj_weight,
    dual_gains,
    out_weight,
    span_bounds,
):
    tok_rows = book_tokens.shape[0]
    seq_devices = lax.axis_size(("seq", "rep"))
    seq_index = lax.axis_index(("seq", "rep"))
    first_row = seq_index * tok_rows
    length = tok_rows * seq_devices
    head_local = query_weight.shape[1] // DH
    normed = normalize(book_tokens.astype(jnp.float32), norm_gain).astype(jnp.bfloat16)
    queries = jnp.dot(normed, query_weight, preferred_element_type=jnp.float32).astype(jnp.bfloat16)
    queries = queries.reshape(tok_rows, head_local, DH)
    key_raw = jnp.dot(normed, key_weight, preferred_element_type=jnp.float32).reshape(
        tok_rows, head_local, DH
    )
    value_raw = jnp.dot(normed, value_weight, preferred_element_type=jnp.float32).reshape(
        tok_rows, head_local, DH
    )
    gain_rows = dual_gains.reshape(4, head_local, DH)
    near_pairs = jnp.concatenate(
        [normalize(key_raw, gain_rows[0]), normalize(value_raw, gain_rows[1])], axis=-1
    )
    near_pairs = near_pairs.astype(jnp.bfloat16)
    raw_pairs = jnp.concatenate([key_raw, value_raw], axis=-1).astype(jnp.bfloat16)
    logits = jnp.dot(normed, proj_weight, preferred_element_type=jnp.float32)
    proj_weights = jnp.exp(capped(logits)).astype(jnp.bfloat16).reshape(tok_rows, head_local, R)
    numerator = jnp.einsum(
        "nhr,nhe->hre", proj_weights, raw_pairs, preferred_element_type=jnp.float32
    )
    flat_pairs = near_pairs.reshape(tok_rows, head_local * 2 * DH)
    padded = with_halo(flat_pairs, ((("seq", "rep"), 0),), SEG // 2)
    segments = tok_rows // SEG
    blocks = padded.reshape(segments + 1, SEG, head_local, 2 * DH)
    window = jnp.concatenate([blocks[:-1], blocks[1:]], axis=1)
    position = (
        first_row + jnp.arange(segments)[:, None] * SEG + jnp.arange(2 * SEG)[None, :] - SEG // 2
    )
    inside = (position >= 0) & (position < length)
    query_blocks = queries.reshape(segments, SEG, head_local, DH)
    near_scores = jnp.einsum(
        "sqhd,skhd->shqk", query_blocks, window[..., :DH], preferred_element_type=jnp.float32
    )
    near_exp = jnp.where(inside[:, None, None, :], jnp.exp(capped(near_scores * DH ** (-0.5))), 0.0)
    total_numer = lax.psum(numerator.astype(jnp.bfloat16), ("seq", "rep")).astype(jnp.float32)
    land_pairs = finish(total_numer, gain_rows)
    far_scores = jnp.einsum(
        "sqhd,hrd->shqr", query_blocks, land_pairs[..., :DH], preferred_element_type=jnp.float32
    )
    far_exp = jnp.exp(capped(far_scores * DH ** (-0.5)))
    summed = jnp.sum(near_exp, axis=-1, keepdims=True) + jnp.sum(far_exp, axis=-1, keepdims=True)
    near_probs = (near_exp / summed).astype(jnp.bfloat16)
    far_probs = (far_exp / summed).astype(jnp.bfloat16)
    output = jnp.einsum(
        "shqk,skhd->sqhd", near_probs, window[..., DH:], preferred_element_type=jnp.float32
    )
    output = output + jnp.einsum(
        "shqr,hrd->sqhd", far_probs, land_pairs[..., DH:], preferred_element_type=jnp.float32
    )
    heads_out = output.astype(jnp.bfloat16).reshape(tok_rows, head_local * DH)
    projected = jnp.dot(
        lax.all_gather(heads_out, "head", axis=1, tiled=True),
        out_weight,
        preferred_element_type=jnp.float32,
    )
    attended = projected.astype(jnp.bfloat16)
    span_start = span_bounds[:, 0]
    span_end = span_bounds[:, 1]
    position_rows = first_row + jnp.arange(tok_rows)
    member = (position_rows[None, :] >= span_start[:, None]) & (
        position_rows[None, :] < span_end[:, None]
    )
    partial_sums = jnp.dot(
        member.astype(jnp.bfloat16), attended, preferred_element_type=jnp.float32
    )
    own_sums = lax.psum_scatter(
        partial_sums.astype(jnp.bfloat16), ("seq", "rep"), scatter_dimension=0, tiled=True
    ).astype(jnp.float32)
    span_rows = own_sums.shape[0]
    own_bounds = lax.dynamic_slice_in_dim(span_bounds, seq_index * span_rows, span_rows, 0)
    own_counts = (own_bounds[:, 1] - own_bounds[:, 0]).astype(jnp.float32)
    pooled = own_sums / own_counts[:, None]
    return (attended, pooled)


def solution(mesh):
    placed = (
        P(("groups", "seq", "rep"), None),
        P(),
        P(None, "head"),
        P(None, "head"),
        P(None, "head"),
        P(None, "head"),
        P(None, "head"),
        P(None, "head"),
        P("groups", None),
    )
    return jax.shard_map(
        per_device,
        mesh=mesh,
        in_specs=placed,
        out_specs=(P(("groups", "seq", "rep"), "head"), P(("groups", "seq", "rep"), "head")),
        check_vma=False,
    )
```

profile of v0, /device:TPU:0, one launch (start us, length us, event | category | flops | bytes accessed | tf_op | source)
XLA Modules:
  0.0 200.5 jit_solution(12161471431930354215)
XLA Ops:
  7.2 2.1 %convert_reduce_fusion = f32[1024]{0:T(1024)S(1)} fusion(bf16[1024,1024]{1,0:T(8,128)(2,1)} %param.9), kind=kLoop, calls=%fused_computation.9 | loop fusion | flops 2096128 | bytes 2101248 | tf_op jit(solution)/shard_map/reduce_sum | solution.py:31
  10.9 2.3 %bitcast_convert_fusion = (bf16[1024,8,64]{0,2,1:T(8,128)(2,1)}, f32[1024,512]{0,1:T(8,128)S(1)}) fusion(bf16[1024,1024]{1,0:T(8,128)(2,1)S(1)} %fusion.6, bf16[1024,512]{1,0:T(8,128)(2,1)S(1)} %copy-done), kind=kOutput, calls=%fused_computation.34 | convolution fusion | flops 1074266112 | bytes 6291456 | tf_op jit(solution)/shard_map/dot_general | solution.py:69
  14.4 2.3 %bitcast_convert_fusion.1 = (bf16[1024,8,64]{0,2,1:T(8,128)(2,1)}, f32[1024,512]{0,1:T(8,128)S(1)}) fusion(bf16[1024,1024]{1,0:T(8,128)(2,1)S(1)} %fusion.6, bf16[1024,512]{1,0:T(8,128)(2,1)S(1)} %copy-done.15), kind=kOutput, calls=%fused_computation.37 | convolution fusion | flops 1074266112 | bytes 6291456 | tf_op jit(solution)/shard_map/dot_general | solution.py:66
  18.3 2.2 %multiply_multiply_fusion = (bf16[1024,8,64]{0,2,1:T(8,128)(2,1)S(1)}, bf16[1024,8,64]{0,2,1:T(8,128)(2,1)S(1)}) fusion(f32[1024,512]{0,1:T(8,128)S(1)} %get-tuple-element.17, f32[8,64]{1,0:T(8,128)S(1)} %mul.128, f32[1024,8]{0,1:T(8,128)S(1)} %add_rsqrt_fusion, f32[1024,8]{0,1:T(8,128)S(1)} %broadcast_multiply_fusion, f32[8,64]{1,0:T(8,128)S(1)} %mul.123, ...), kind=kLoop, calls=%fused_computation.40 | loop fusion | flops 4194304 | bytes 6426624 | tf_op jit(solution)/shard_map/mul | solution.py:33
  21.0 2.4 %collective-permute-start = (bf16[64,1024]{1,0:T(8,128)(2,1)S(1)}, bf16[64,1024]{1,0:T(8,128)(2,1)S(1)}, u32[]{:S(2)}, u32[]{:S(2)}) collective-permute-start(bf16[64,1024]{1,0:T(8,128)(2,1)S(1)} %copy.38), channel_id=1, source_target_pairs={{0,1},{1,4},{4,5},{5,8},{8,9},{9,12},{12,13},{2,3},{3,6},{6,7},{7,... | collective-permute-start | bytes 393224 | tf_op jit(solution)/shard_map/ppermute | solution.py:21
  25.6 9.9 %exponential_convert_fusion = bf16[1024,2048]{1,0:T(8,128)(2,1)} fusion(bf16[1024,1024]{1,0:T(8,128)(2,1)} %copy-done.6, bf16[1024,2048]{1,0:T(8,128)(2,1)} %param.14), kind=kOutput, calls=%fused_computation.5 | convolution fusion | flops 4301258752 | bytes 10485760 | tf_op jit(solution)/shard_map/dot_general | solution.py:78
  35.6 6.5 %copy.58 = bf16[1024,2048]{0,1:T(8,128)(2,1)} copy(bf16[1024,2048]{1,0:T(8,128)(2,1)} %exponential_convert_fusion) | data formatting | bytes 8388608 | tf_op jit(solution)/shard_map/reshape | solution.py:79
  42.1 4.5 %fusion.23 = bf16[8,256,128]{2,1,0:T(8,128)(2,1)} fusion(bf16[1024,8,256]{0,2,1:T(8,128)(2,1)} %bitcast.78, bf16[1024,8,64]{0,2,1:T(8,128)(2,1)S(1)} %copy-done.17, bf16[1024,8,64]{0,2,1:T(8,128)(2,1)} %get-tuple-element.18), kind=kOutput, calls=%fused_computation.46 | convolution fusion | flops 541327360 | bytes 6815744 | tf_op jit(solution)/shard_map/nhr,nhe->hre/dot_general | solution.py:80
  46.9 2.6 %copy.39 = bf16[1024,1024]{1,0:T(8,128)(2,1)} copy(bf16[1024,1024]{0,1:T(8,128)(2,1)S(1)} %bitcast.75) | data formatting | bytes 4194304 | tf_op jit(solution)/shard_map/convert_element_type | solution.py:76
  49.5 3.1 %convolution_convert_fusion.1 = bf16[1024,512]{1,0:T(8,128)(2,1)S(1)} fusion(bf16[1024,1024]{1,0:T(8,128)(2,1)} %copy-done.6, bf16[1024,512]{1,0:T(8,128)(2,1)} %param.11), kind=kOutput, calls=%fused_computation.45 | convolution fusion | flops 1074266112 | bytes 4194304 | tf_op jit(solution)/shard_map/dot_general | solution.py:64
  52.6 2.1 %reshape.140 = bf16[8,128,8,64]{3,2,1,0:T(8,128)(2,1)} reshape(bf16[1024,512]{1,0:T(8,128)(2,1)S(1)} %convolution_convert_fusion.1) | data formatting | bytes 2097152 | tf_op jit(solution)/shard_map/reshape;reshape | solution.py:92
  54.7 2.4 %copy.45 = bf16[8,128,8,64]{1,3,2,0:T(8,128)(2,1)S(1)} copy(bf16[8,128,8,64]{3,2,1,0:T(8,128)(2,1)} %reshape.140) | data formatting | bytes 2097152 | tf_op jit(solution)/shard_map/reshape;reshape | solution.py:92
  59.3 2.0 copy.64
  61.2 4.3 %copy.42 = bf16[8,128,8,128]{1,3,2,0:T(8,128)(2,1)} copy(bf16[8,128,8,128]{3,2,1,0:T(8,128)(2,1)} %bitcast.76) | data formatting | bytes 4194304 | tf_op jit(solution)/shard_map/slice | solution.py:87
  65.5 1.9 copy.65
  67.5 4.3 %copy.43 = bf16[8,128,8,128]{1,3,2,0:T(8,128)(2,1)} copy(bf16[8,128,8,128]{3,2,1,0:T(8,128)(2,1)} %bitcast.77) | data formatting | bytes 4194304 | tf_op jit(solution)/shard_map/slice | solution.py:87
  71.7 7.5 %fusion.1 = (f32[8,8,128]{2,1,0:T(8,128)S(1)}, f32[8,8,128,256]{3,2,1,0:T(8,128)}) fusion(pred[8,256]{1,0:T(8,128)(4,1)S(1)} %fusion.45, bf16[8,128,8,64]{1,3,2,0:T(8,128)(2,1)S(1)} %copy.45, bf16[8,128,8,128]{1,3,2,0:T(8,128)(2,1)} %copy.43, bf16[8,128,8,128]{1,3,2,0:T(8,128)(2,1)S(1)} %copy-done.7), kind=kOutput, calls=%fused_computation.7 | convolution fusion | flops 281010176 | bytes 13666304 | tf_op jit(solution)/shard_map/sqhd,skhd->shqk/dot_general | solution.py:93
  79.2 28.3 %all-reduce.2.cloned.1.call-done = bf16[8,256,128]{2,1,0:T(8,128)(2,1)} async-done(((bf16[8,256,128]{2,1,0:T(8,128)(2,1)}), bf16[8,256,128]{2,1,0:T(8,128)(2,1)}) %all-reduce.2.cloned.1.call-update) | async-done | bytes 524304 | tf_op jit(solution)/shard_map/psum | solution.py:97
  111.2 3.9 %bitcast_reduce_fusion = (f32[8,8,128]{2,1,0:T(8,128)S(1)}, f32[8,256,8,128]{1,3,0,2:T(8,128)S(1)}) fusion(bf16[8,128,8,64]{1,3,2,0:T(8,128)(2,1)S(1)} %copy-done.10, f32[8,256,128]{2,1,0:T(8,128)S(1)} %convert_element_type.57, f32[8,64]{1,0:T(8,128)S(1)} %mul.138, f32[8,256]{1,0:T(8,128)S(1)} %add_rsqrt_fusion.3, f32[8,256]{1,0:T(8,128)S(1)} %get-tuple-element.25), kind=kOutput, calls=%fused_computation.1 | convolution fusion | flops 275243008 | bytes 10536960 | tf_op jit(solution)/shard_map/sqhd,hrd->shqr/dot_general | solution.py:99
  115.2 5.2 %fusion.8 = f32[8,64,8,128]{3,1,0,2:T(8,128)S(1)} fusion(f32[8,256,8,128]{1,3,0,2:T(8,128)S(1)} %get-tuple-element.23, f32[8,8,128]{2,1,0:T(8,128)S(1)} %add.118, f32[8,256,128]{2,1,0:T(8,128)S(1)} %convert_element_type.57, f32[8,64]{1,0:T(8,128)S(1)} %mul.144, f32[8,256]{1,0:T(8,128)S(1)} %add_rsqrt_fusion.2, f32[8,256]{1,0:T(8,128)S(1)} %get-tuple-element.24), kind=kOutput, calls=%fused_computation.19 | convolution fusion | flops 277348352 | bytes 11585536 | tf_op jit(solution)/shard_map/shqr,hrd->sqhd/dot_general | solution.py:109
  120.4 3.8 %fusion.20 = bf16[8,128,8,64]{1,3,2,0:T(8,128)(2,1)S(1)} fusion(f32[8,64,8,128]{3,1,0,2:T(8,128)S(1)} %fusion.8, f32[8,8,128,256]{3,2,1,0:T(8,128)S(1)} %bitcast.84, f32[8,8,128]{2,1,0:T(8,128)S(1)} %add.118, pred[8,256]{1,0:T(8,128)(4,1)S(1)} %fusion.45, bf16[8,128,8,128]{1,3,2,0:T(8,128)(2,1)S(1)} %copy-done.7, bf16[8,128,8,128]{1,3,2,0:T(8,128)(2,1)S(1)} %copy-done.8), kind=kOutput, calls=%fused_computation.33 | convolution fusion | flops 284164096 | bytes 15763456 | tf_op jit(solution)/shard_map/shqk,skhd->sqhd/dot_general | solution.py:106
  126.3 32.1 %all-gather.2.cloned.1.call-done = bf16[1024,1024]{0,1:T(8,128)(2,1)} async-done(((bf16[1024,512]{0,1:T(8,128)(2,1)}), bf16[1024,1024]{0,1:T(8,128)(2,1)}) %all-gather.2.cloned.1.call-update) | async-done | bytes 2097168 | tf_op jit(solution)/shard_map/all_gather | solution.py:114
  158.4 3.0 %convolution_convert_fusion = bf16[1024,512]{1,0:T(8,128)(2,1)S(1)} fusion(bf16[1024,1024]{0,1:T(8,128)(2,1)} %all-gather.2.cloned.1.call-done, bf16[1024,512]{1,0:T(8,128)(2,1)S(1)} %copy-done.16), kind=kOutput, calls=%fused_computation.44 | convolution fusion | flops 1074266112 | bytes 4194304 | tf_op jit(solution)/shard_map/dot_general | solution.py:113
  162.4 30.2 %reduce-scatter.2.cloned.1.call-done = bf16[8,512]{1,0:T(8,128)(2,1)} async-done(((bf16[64,512]{1,0:T(8,128)(2,1)}), bf16[8,512]{1,0:T(8,128)(2,1)}) %reduce-scatter.2.cloned.1.call-update) | async-done | bytes 8208 | tf_op jit(solution)/shard_map/reduce_scatter | solution.py:128
  (89 shorter events, 17.6 us)
Async XLA Ops:
  7.2 3.7 %copy-start = (bf16[1024,512]{1,0:T(8,128)(2,1)S(1)}, bf16[1024,512]{1,0:T(8,128)(2,1)}, u32[]{:S(2)}) copy-start(bf16[1024,512]{1,0:T(8,128)(2,1)} %param.13) | copy-start | bytes 3145732
  7.2 2.3 %copy-start.2 = (bf16[1024,1024]{1,0:T(8,128)(2,1)S(1)}, bf16[1024,1024]{1,0:T(8,128)(2,1)}, u32[]{:S(2)}) copy-start(bf16[1024,1024]{1,0:T(8,128)(2,1)} %param.9) | copy-start | bytes 6291460
  7.2 3.0 %copy-start.13 = (f32[1024]{0:T(1024)S(1)}, f32[1024]{0:T(1024)}, u32[]{:S(2)}) copy-start(f32[1024]{0:T(1024)} %param.10) | copy-start | bytes 12292
  7.2 100.3 %all-reduce.2.cloned.1.call-start = ((), (), s32[]{:S(2)}) async-start(), calls=%async_computation.1 | async-start | bytes 1048576 | tf_op jit(solution)/shard_map/psum | solution.py:97
  10.9 2.9 %copy-start.6 = (bf16[1024,1024]{1,0:T(8,128)(2,1)}, bf16[1024,1024]{1,0:T(8,128)(2,1)S(1)}, u32[]{:S(2)}) copy-start(bf16[1024,1024]{1,0:T(8,128)(2,1)S(1)} %fusion.6) | copy-start | bytes 6291460
  16.7 1.4 copy-start.3
  16.7 1.4 copy-start.12
  21.0 36.3 %collective-permute-start = (bf16[64,1024]{1,0:T(8,128)(2,1)S(1)}, bf16[64,1024]{1,0:T(8,128)(2,1)S(1)}, u32[]{:S(2)}, u32[]{:S(2)}) collective-permute-start(bf16[64,1024]{1,0:T(8,128)(2,1)S(1)} %copy.38), channel_id=1, source_target_pairs={{0,1},{1,4},{4,5},{5,8},{8,9},{9,12},{12,13},{2,3},{3,6},{6,7},{7,... | collective-permute-start | bytes 393224 | tf_op jit(solution)/shard_map/ppermute | solution.py:21
  24.2 33.2 %collective-permute-start.1 = (bf16[64,1024]{1,0:T(8,128)(2,1)}, bf16[64,1024]{1,0:T(8,128)(2,1)S(1)}, u32[]{:S(2)}, u32[]{:S(2)}) collective-permute-start(bf16[64,1024]{1,0:T(8,128)(2,1)} %copy.40), channel_id=1, source_target_pairs={{1,0},{4,1},{5,4},{8,5},{9,8},{12,9},{13,12},{3,2},{6,3},{7,6},{10... | collective-permute-start | bytes 393224 | tf_op jit(solution)/shard_map/ppermute | solution.py:23
  35.6 6.5 %copy-start.17 = (bf16[1024,8,64]{0,2,1:T(8,128)(2,1)S(1)}, bf16[1024,8,64]{0,2,1:T(8,128)(2,1)}, u32[]{:S(2)}) copy-start(bf16[1024,8,64]{0,2,1:T(8,128)(2,1)} %get-tuple-element.16) | copy-start | bytes 3145732
  46.6 111.8 %all-gather.2.cloned.1.call-start = ((), (), s32[]{:S(2)}) async-start(), calls=%async_computation.2 | async-start | bytes 3145728 | tf_op jit(solution)/shard_map/all_gather | solution.py:114
  54.7 2.7 %copy-start.4 = (bf16[1024,1024]{1,0:T(8,128)(2,1)S(1)}, bf16[1024,1024]{1,0:T(8,128)(2,1)}, u32[]{:S(2)}) copy-start(bf16[1024,1024]{1,0:T(8,128)(2,1)} %copy.39) | copy-start | bytes 6291460
  57.1 14.6 %copy-start.9 = (bf16[8,128,8,64]{1,3,2,0:T(8,128)(2,1)}, bf16[8,128,8,64]{1,3,2,0:T(8,128)(2,1)S(1)}, u32[]{:S(2)}) copy-start(bf16[8,128,8,64]{1,3,2,0:T(8,128)(2,1)S(1)} %copy.45) | copy-start | bytes 3145732
  61.2 4.3 %copy-start.5 = (bf16[128,8,8,128]{3,1,2,0:T(8,128)(2,1)S(1)}, bf16[128,8,8,128]{3,1,2,0:T(8,128)(2,1)}, u32[]{:S(2)}) copy-start(bf16[128,8,8,128]{3,1,2,0:T(8,128)(2,1)} %get-tuple-element.11) | copy-start | bytes 6291460
  67.5 4.3 %copy-start.7 = (bf16[8,128,8,128]{1,3,2,0:T(8,128)(2,1)S(1)}, bf16[8,128,8,128]{1,3,2,0:T(8,128)(2,1)}, u32[]{:S(2)}) copy-start(bf16[8,128,8,128]{1,3,2,0:T(8,128)(2,1)} %copy.42) | copy-start | bytes 6291460
  108.6 2.5 %copy-start.10 = (bf16[8,128,8,64]{1,3,2,0:T(8,128)(2,1)S(1)}, bf16[8,128,8,64]{1,3,2,0:T(8,128)(2,1)}, u32[]{:S(2)}) copy-start(bf16[8,128,8,64]{1,3,2,0:T(8,128)(2,1)} %copy-done.9) | copy-start | bytes 3145732
  111.2 9.2 %slice-start = ((s8[8388608]{0:T(1024)(128)(4,1)}), s8[4194304]{0:T(1024)(128)(4,1)S(1)}, s32[]{:S(2)}) async-start(s8[8388608]{0:T(1024)(128)(4,1)} %bitcast.83), calls=%async_computation.4 | async-start | bytes 8388608
  115.2 5.2 %copy-start.8 = (bf16[8,128,8,128]{1,3,2,0:T(8,128)(2,1)S(1)}, bf16[8,128,8,128]{1,3,2,0:T(8,128)(2,1)}, u32[]{:S(2)}) copy-start(bf16[8,128,8,128]{1,3,2,0:T(8,128)(2,1)} %copy.43) | copy-start | bytes 6291460
  115.2 5.2 %slice-start.1 = ((s8[8388608]{0:T(1024)(128)(4,1)}), s8[4194304]{0:T(1024)(128)(4,1)S(1)}, s32[]{:S(2)}) async-start(s8[8388608]{0:T(1024)(128)(4,1)} %bitcast.83), calls=%async_computation.5 | async-start | bytes 8388608
  124.8 1.4 copy-start.14
  124.9 33.5 %copy-start.16 = (bf16[1024,512]{1,0:T(8,128)(2,1)S(1)}, bf16[1024,512]{1,0:T(8,128)(2,1)}, u32[]{:S(2)}) copy-start(bf16[1024,512]{1,0:T(8,128)(2,1)} %param.16) | copy-start | bytes 3145732
  126.1 66.4 %reduce-scatter.2.cloned.1.call-start = ((), (), s32[]{:S(2)}) async-start(), calls=%async_computation.3 | async-start | bytes 73728 | tf_op jit(solution)/shard_map/reduce_scatter | solution.py:128
  158.4 35.6 %copy-start.1 = (bf16[1024,512]{1,0:T(8,128)(2,1)S(1)}, bf16[1024,512]{1,0:T(8,128)(2,1)}, u32[]{:S(2)}) copy-start(bf16[1024,512]{1,0:T(8,128)(2,1)} %param.13) | copy-start | bytes 3145732
  161.4 32.6 %copy-start.11 = (bf16[1024,512]{1,0:T(8,128)(2,1)}, bf16[1024,512]{1,0:T(8,128)(2,1)S(1)}, u32[]{:S(2)}) copy-start(bf16[1024,512]{1,0:T(8,128)(2,1)S(1)} %convolution_convert_fusion) | copy-start | bytes 3145732
  (1 other events, 1.2 us)
Sparse Core Ops, SparseCore 0:
  46.8 60.7 all-reduce.1
  126.3 32.0 all-gather.1
  162.5 30.0 reduce-scatter.1
where the time goes:
time: 201 us; the launch traced here: 200 us
  waiting for transfers between devices  90.6 us (45%)
  matrix products  46.4 us (23%)
  local copies, waits for them, and re-layouts  31.1 us (15%)
  between operations  14.2 us (7%)
  other arithmetic  14 us (7%)
  starting transfers between devices  4.17 us (2%)
    all_gather x1, waiting for transfers between devices, per_device(): lax.all_gather(heads_out, 'head', axis=1, tiled=True)  32.1 us
    reduce_scatter x1, waiting for transfers between devices, per_device(): lax.psum_scatter(partial_sums.astype(jnp.bfloat16), ('seq', 'rep'), scatt...  30.2 us
    psum x1, waiting for transfers between devices, per_device(): lax.psum(numerator.astype(jnp.bfloat16), ('seq', 'rep')).astype(jnp.float32)  28.3 us
    dot_general x1, matrix products, per_device(): logits = jnp.dot(normed, proj_weight, preferred_element_type=jnp.float32)  9.95 us
    slice x2, local copies, waits for them, and re-layouts, per_device(): window = jnp.concatenate([blocks[:-1], blocks[1:]], axis=1)  8.56 us
    dot_general x1, matrix products, per_device(): jnp.einsum('sqhd,skhd->shqk', query_blocks, window[..., :DH], preferred_e...  7.46 us
    unnamed x43, local copies, waits for them, and re-layouts  6.76 us
    reshape x1, local copies, waits for them, and re-layouts, per_device(): jnp.exp(capped(logits)).astype(jnp.bfloat16)  6.49 us
  transfers between devices with their start and end apart: 5, of which 3 were waited for; matrix products, arithmetic and copies ran while one was open for 27% of the time, Pallas kernels for 0%

commit v1 on v0

--- a/solution.py
+++ b/solution.py
@@ -94,7 +94,9 @@
         "sqhd,skhd->shqk", query_blocks, window[..., :DH], preferred_element_type=jnp.float32
     )
     near_exp = jnp.where(inside[:, None, None, :], jnp.exp(capped(near_scores * DH ** (-0.5))), 0.0)
-    total_numer = lax.psum(numerator.astype(jnp.bfloat16), ("seq", "rep")).astype(jnp.float32)
+    total_numer = jnp.sum(
+        lax.all_gather(numerator.astype(jnp.bfloat16), ("seq", "rep")), axis=0
+    ).astype(jnp.float32)
     land_pairs = finish(total_numer, gain_rows)
     far_scores = jnp.einsum(
         "sqhd,hrd->shqr", query_blocks, land_pairs[..., :DH], preferred_element_type=jnp.float32

time: 201 us -> 181 us (0.900)
  waiting for transfers between devices: 90.6 us -> 72.4 us
    psum x1 -> x0, waiting for transfers between devices: 28.3 us -> none  [per_device(): lax.psum(numerator.astype(jnp.bfloat16), ('seq', 'rep')).astype(jnp.float32)]
    all_gather x0 -> x1, waiting for transfers between devices: none -> 10.3 us  [per_device(): lax.all_gather(numerator.astype(jnp.bfloat16), ('seq', 'rep'))]
    dot_general x1, matrix products: 9.95 us -> 6.89 us  [per_device(): logits = jnp.dot(normed, proj_weight, preferred_element_type=jnp.float32)]
    reduce_sum x0 -> x1, other arithmetic: none -> 2.94 us  [per_device(): jnp.sum(lax.all_gather(numerator.astype(jnp.bfloat16), ('seq', 'rep')), a...]
    unnamed x43 -> x45, local copies, waits for them, and re-layouts: 6.76 us -> 6.75 us
  transfers between devices with their start and end apart: 5 -> 5, of which waited for: 3 -> 3; matrix products, arithmetic and copies ran while one was open for 27% -> 20% of each run, Pallas kernels for 0% -> 0%
where the time goes in v1:
time: 181 us
  waiting for transfers between devices  72.4 us (40%)
  matrix products  44.9 us (25%)
  local copies, waits for them, and re-layouts  31 us (17%)
  other arithmetic  14.4 us (8%)
  between operations  14.2 us (8%)
  starting transfers between devices  3.94 us (2%)
    all_gather x1, waiting for transfers between devices, per_device(): lax.all_gather(heads_out, 'head', axis=1, tiled=True)  31.8 us
    reduce_scatter x1, waiting for transfers between devices, per_device(): lax.psum_scatter(partial_sums.astype(jnp.bfloat16), ('seq', 'rep'), scatt...  30.2 us
    all_gather x1, waiting for transfers between devices, per_device(): lax.all_gather(numerator.astype(jnp.bfloat16), ('seq', 'rep'))  10.3 us
    slice x2, local copies, waits for them, and re-layouts, per_device(): window = jnp.concatenate([blocks[:-1], blocks[1:]], axis=1)  8.61 us
    dot_general x1, matrix products, per_device(): jnp.einsum('sqhd,skhd->shqk', query_blocks, window[..., :DH], preferred_e...  7.47 us
    dot_general x1, matrix products, per_device(): logits = jnp.dot(normed, proj_weight, preferred_element_type=jnp.float32)  6.89 us
    unnamed x45, local copies, waits for them, and re-layouts  6.75 us
    reshape x1, local copies, waits for them, and re-layouts, per_device(): jnp.exp(capped(logits)).astype(jnp.bfloat16)  6.4 us
  transfers between devices with their start and end apart: 5, of which 3 were waited for; matrix products, arithmetic and copies ran while one was open for 20% of the time, Pallas kernels for 0%

profile of v1, /device:TPU:0, one launch (start us, length us, event | category | flops | bytes accessed | tf_op | source)
XLA Modules:
  0.0 180.8 jit_solution(7487133293092711144)
XLA Ops:
  7.2 2.1 %convert_reduce_fusion = f32[1024]{0:T(1024)S(1)} fusion(bf16[1024,1024]{1,0:T(8,128)(2,1)} %param.9), kind=kLoop, calls=%fused_computation.9 | loop fusion | flops 2096128 | bytes 2101248 | tf_op jit(solution)/shard_map/reduce_sum | solution.py:31
  10.9 2.3 %bitcast_convert_fusion = (bf16[1024,8,64]{0,2,1:T(8,128)(2,1)}, f32[1024,512]{0,1:T(8,128)S(1)}) fusion(bf16[1024,1024]{1,0:T(8,128)(2,1)S(1)} %fusion.6, bf16[1024,512]{1,0:T(8,128)(2,1)S(1)} %copy-done), kind=kOutput, calls=%fused_computation.34 | convolution fusion | flops 1074266112 | bytes 6291456 | tf_op jit(solution)/shard_map/dot_general | solution.py:69
  13.2 3.2 %bitcast_convert_fusion.1 = (bf16[1024,8,64]{0,2,1:T(8,128)(2,1)}, f32[1024,512]{0,1:T(8,128)}) fusion(bf16[1024,1024]{1,0:T(8,128)(2,1)S(1)} %fusion.6, bf16[1024,512]{1,0:T(8,128)(2,1)S(1)} %copy-done.17), kind=kOutput, calls=%fused_computation.37 | convolution fusion | flops 1074266112 | bytes 6291456 | tf_op jit(solution)/shard_map/dot_general | solution.py:66
  16.4 6.9 %exponential_convert_fusion = bf16[1024,2048]{1,0:T(8,128)(2,1)} fusion(bf16[1024,1024]{1,0:T(8,128)(2,1)S(1)} %fusion.6, bf16[1024,2048]{1,0:T(8,128)(2,1)S(1)} %copy-done.16), kind=kOutput, calls=%fused_computation.5 | convolution fusion | flops 4301258752 | bytes 10485760 | tf_op jit(solution)/shard_map/dot_general | solution.py:78
  23.3 6.4 %copy.69 = bf16[1024,2048]{0,1:T(8,128)(2,1)} copy(bf16[1024,2048]{1,0:T(8,128)(2,1)} %exponential_convert_fusion) | data formatting | bytes 8388608 | tf_op jit(solution)/shard_map/reshape | solution.py:79
  29.7 4.8 %fusion.23 = bf16[8,256,128]{2,1,0:T(8,128)(2,1)} fusion(bf16[1024,8,256]{0,2,1:T(8,128)(2,1)} %bitcast.80, bf16[1024,8,64]{0,2,1:T(8,128)(2,1)} %get-tuple-element.16, bf16[1024,8,64]{0,2,1:T(8,128)(2,1)} %get-tuple-element.18), kind=kOutput, calls=%fused_computation.46 | convolution fusion | flops 541327360 | bytes 6815744 | tf_op jit(solution)/shard_map/nhr,nhe->hre/dot_general | solution.py:80
  38.5 2.4 %collective-permute-start = (bf16[64,1024]{1,0:T(8,128)(2,1)S(1)}, bf16[64,1024]{1,0:T(8,128)(2,1)S(1)}, u32[]{:S(2)}, u32[]{:S(2)}) collective-permute-start(bf16[64,1024]{1,0:T(8,128)(2,1)S(1)} %copy.49), channel_id=1, source_target_pairs={{0,1},{1,4},{4,5},{5,8},{8,9},{9,12},{12,13},{2,3},{3,6},{6,7},{7,... | collective-permute-start | bytes 393224 | tf_op jit(solution)/shard_map/ppermute | solution.py:21
  43.1 2.6 %copy.50 = bf16[1024,1024]{1,0:T(8,128)(2,1)} copy(bf16[1024,1024]{0,1:T(8,128)(2,1)S(1)} %bitcast.76) | data formatting | bytes 4194304 | tf_op jit(solution)/shard_map/convert_element_type | solution.py:76
  45.7 3.2 %convolution_convert_fusion.1 = bf16[1024,512]{1,0:T(8,128)(2,1)S(1)} fusion(bf16[1024,1024]{1,0:T(8,128)(2,1)} %copy-done.6, bf16[1024,512]{1,0:T(8,128)(2,1)} %param.11), kind=kOutput, calls=%fused_computation.45 | convolution fusion | flops 1074266112 | bytes 4194304 | tf_op jit(solution)/shard_map/dot_general | solution.py:64
  48.9 2.1 %reshape.141 = bf16[8,128,8,64]{3,2,1,0:T(8,128)(2,1)} reshape(bf16[1024,512]{1,0:T(8,128)(2,1)S(1)} %convolution_convert_fusion.1) | data formatting | bytes 2097152 | tf_op jit(solution)/shard_map/reshape;reshape | solution.py:92
  51.0 2.4 %copy.56 = bf16[8,128,8,64]{1,3,2,0:T(8,128)(2,1)S(1)} copy(bf16[8,128,8,64]{3,2,1,0:T(8,128)(2,1)} %reshape.141) | data formatting | bytes 2097152 | tf_op jit(solution)/shard_map/reshape;reshape | solution.py:92
  53.7 2.0 %fusion.15 = (bf16[128,8,8,128]{3,1,2,0:T(8,128)(2,1)S(1)}, bf16[128,8,8,128]{3,1,2,0:T(8,128)(2,1)}) fusion(bf16[1024,1024]{1,0:T(8,128)(2,1)S(1)} %copy-done.4, bf16[64,1024]{1,0:T(8,128)(2,1)S(1)} %collective-permute-done, bf16[64,1024]{1,0:T(8,128)(2,1)S(1)} %collective-permute-done.1), kind=kLoop, calls=%fused_computation.27 | loop fusion | flops 8388608 | bytes 6553600
  57.6 4.3 %copy.53 = bf16[8,128,8,128]{1,3,2,0:T(8,128)(2,1)} copy(bf16[8,128,8,128]{3,2,1,0:T(8,128)(2,1)} %bitcast.77) | data formatting | bytes 4194304 | tf_op jit(solution)/shard_map/slice | solution.py:87
  61.9 2.0 %copy.76 = bf16[128,8,8,128]{3,2,1,0:T(8,128)(2,1)} copy(bf16[128,8,8,128]{3,1,2,0:T(8,128)(2,1)S(1)} %copy-done.5) | data formatting | bytes 4194304
  63.8 4.3 %copy.54 = bf16[8,128,8,128]{1,3,2,0:T(8,128)(2,1)} copy(bf16[8,128,8,128]{3,2,1,0:T(8,128)(2,1)} %bitcast.78) | data formatting | bytes 4194304 | tf_op jit(solution)/shard_map/slice | solution.py:87
  68.2 7.5 %fusion.1 = (f32[8,8,128]{2,1,0:T(8,128)S(1)}, f32[8,8,128,256]{3,2,1,0:T(8,128)}) fusion(pred[8,256]{1,0:T(8,128)(4,1)S(1)} %fusion.45, bf16[8,128,8,64]{1,3,2,0:T(8,128)(2,1)S(1)} %copy.56, bf16[8,128,8,128]{1,3,2,0:T(8,128)(2,1)} %copy.54, bf16[8,128,8,128]{1,3,2,0:T(8,128)(2,1)S(1)} %copy-done.7), kind=kOutput, calls=%fused_computation.7 | convolution fusion | flops 281010176 | bytes 13666304 | tf_op jit(solution)/shard_map/sqhd,skhd->shqk/dot_general | solution.py:93
  75.6 10.3 %all-gather.6.cloned.1.call-done = bf16[64,256,128]{2,1,0:T(8,128)(2,1)} async-done(((bf16[8,256,128]{2,1,0:T(8,128)(2,1)}), bf16[64,256,128]{2,1,0:T(8,128)(2,1)}) %all-gather.6.cloned.1.call-update) | async-done | bytes 4194320 | tf_op jit(solution)/shard_map/all_gather | solution.py:98
  85.9 2.9 %reduce_sum.127 = bf16[8,256,128]{2,1,0:T(8,128)(2,1)S(1)} reduce(bf16[8,8,256,128]{3,2,1,0:T(8,128)(2,1)} %bitcast.79, bf16[]{:T(256)} %constant.58.clone.1), dimensions={0}, to_apply=%region_7.8 | reduce | flops 1835008 | bytes 4718594 | tf_op jit(solution)/shard_map/reduce_sum | solution.py:97
  91.5 3.9 %bitcast_reduce_fusion = (f32[8,8,128]{2,1,0:T(8,128)S(1)}, f32[8,256,8,128]{1,3,0,2:T(8,128)S(1)}) fusion(bf16[8,128,8,64]{1,3,2,0:T(8,128)(2,1)S(1)} %copy-done.11, f32[8,256,128]{2,1,0:T(8,128)S(1)} %convert_element_type.59, f32[8,64]{1,0:T(8,128)S(1)} %mul.138, f32[8,256]{1,0:T(8,128)S(1)} %add_rsqrt_fusion.3, f32[8,256]{1,0:T(8,128)S(1)} %get-tuple-element.25), kind=kOutput, calls=%fused_computation.1 | convolution fusion | flops 275243008 | bytes 10536960 | tf_op jit(solution)/shard_map/sqhd,hrd->shqr/dot_general | solution.py:101
  95.5 5.2 %fusion.8 = f32[8,64,8,128]{3,1,0,2:T(8,128)S(1)} fusion(f32[8,256,8,128]{1,3,0,2:T(8,128)S(1)} %get-tuple-element.23, f32[8,8,128]{2,1,0:T(8,128)S(1)} %add.116, f32[8,256,128]{2,1,0:T(8,128)S(1)} %convert_element_type.59, f32[8,64]{1,0:T(8,128)S(1)} %mul.144, f32[8,256]{1,0:T(8,128)S(1)} %add_rsqrt_fusion.2, f32[8,256]{1,0:T(8,128)S(1)} %get-tuple-element.24), kind=kOutput, calls=%fused_computation.19 | convolution fusion | flops 277348352 | bytes 11585536 | tf_op jit(solution)/shard_map/shqr,hrd->sqhd/dot_general | solution.py:111
  100.7 4.0 %fusion.20 = bf16[8,128,8,64]{1,3,2,0:T(8,128)(2,1)S(1)} fusion(f32[8,64,8,128]{3,1,0,2:T(8,128)S(1)} %fusion.8, f32[8,8,128,256]{3,2,1,0:T(8,128)S(1)} %bitcast.86, f32[8,8,128]{2,1,0:T(8,128)S(1)} %add.116, pred[8,256]{1,0:T(8,128)(4,1)S(1)} %fusion.45, bf16[8,128,8,128]{1,3,2,0:T(8,128)(2,1)S(1)} %copy-done.8, bf16[8,128,8,128]{1,3,2,0:T(8,128)(2,1)S(1)} %copy-done.9), kind=kOutput, calls=%fused_computation.33 | convolution fusion | flops 284164096 | bytes 15763456 | tf_op jit(solution)/shard_map/shqk,skhd->sqhd/dot_general | solution.py:108
  106.8 31.8 %all-gather.4.cloned.1.call-done = bf16[1024,1024]{0,1:T(8,128)(2,1)} async-done(((bf16[1024,512]{0,1:T(8,128)(2,1)}), bf16[1024,1024]{0,1:T(8,128)(2,1)}) %all-gather.4.cloned.1.call-update) | async-done | bytes 2097168 | tf_op jit(solution)/shard_map/all_gather | solution.py:116
  138.7 3.0 %convolution_convert_fusion = bf16[1024,512]{1,0:T(8,128)(2,1)S(1)} fusion(bf16[1024,1024]{0,1:T(8,128)(2,1)} %all-gather.4.cloned.1.call-done, bf16[1024,512]{1,0:T(8,128)(2,1)S(1)} %copy-done.18), kind=kOutput, calls=%fused_computation.44 | convolution fusion | flops 1074266112 | bytes 4194304 | tf_op jit(solution)/shard_map/dot_general | solution.py:115
  142.7 30.2 %reduce-scatter.2.cloned.1.call-done = bf16[8,512]{1,0:T(8,128)(2,1)} async-done(((bf16[64,512]{1,0:T(8,128)(2,1)}), bf16[8,512]{1,0:T(8,128)(2,1)}) %reduce-scatter.2.cloned.1.call-update) | async-done | bytes 8208 | tf_op jit(solution)/shard_map/reduce_scatter | solution.py:130
  (92 shorter events, 17.0 us)
Async XLA Ops:
  7.2 3.7 %copy-start = (bf16[1024,512]{1,0:T(8,128)(2,1)S(1)}, bf16[1024,512]{1,0:T(8,128)(2,1)}, u32[]{:S(2)}) copy-start(bf16[1024,512]{1,0:T(8,128)(2,1)} %param.13) | copy-start | bytes 3145732
  7.2 2.3 %copy-start.2 = (bf16[1024,1024]{1,0:T(8,128)(2,1)S(1)}, bf16[1024,1024]{1,0:T(8,128)(2,1)}, u32[]{:S(2)}) copy-start(bf16[1024,1024]{1,0:T(8,128)(2,1)} %param.9) | copy-start | bytes 6291460
  7.2 3.0 %copy-start.14 = (f32[1024]{0:T(1024)S(1)}, f32[1024]{0:T(1024)}, u32[]{:S(2)}) copy-start(f32[1024]{0:T(1024)} %param.10) | copy-start | bytes 12292
  7.2 78.7 %all-gather.6.cloned.1.call-start = ((), (), s32[]{:S(2)}) async-start(), calls=%async_computation.3 | async-start | bytes 4718592 | tf_op jit(solution)/shard_map/all_gather | solution.py:98
  10.9 5.5 %copy-start.6 = (bf16[1024,1024]{1,0:T(8,128)(2,1)}, bf16[1024,1024]{1,0:T(8,128)(2,1)S(1)}, u32[]{:S(2)}) copy-start(bf16[1024,1024]{1,0:T(8,128)(2,1)S(1)} %fusion.6) | copy-start | bytes 6291460
  10.9 2.3 %copy-start.17 = (bf16[1024,512]{1,0:T(8,128)(2,1)S(1)}, bf16[1024,512]{1,0:T(8,128)(2,1)}, u32[]{:S(2)}) copy-start(bf16[1024,512]{1,0:T(8,128)(2,1)} %param.12) | copy-start | bytes 3145732
  13.2 3.2 %copy-start.16 = (bf16[1024,2048]{1,0:T(8,128)(2,1)S(1)}, bf16[1024,2048]{1,0:T(8,128)(2,1)}, u32[]{:S(2)}) copy-start(bf16[1024,2048]{1,0:T(8,128)(2,1)} %param.14) | copy-start | bytes 12582916
  29.7 4.9 %copy-start.13 = (f32[4,512]{1,0:T(4,128)S(1)}, f32[4,512]{1,0:T(4,128)}, u32[]{:S(2)}) copy-start(f32[4,512]{1,0:T(4,128)} %param.15) | copy-start | bytes 24580
  34.6 104.1 %all-gather.4.cloned.1.call-start = ((), (), s32[]{:S(2)}) async-start(), calls=%async_computation.1 | async-start | bytes 3145728 | tf_op jit(solution)/shard_map/all_gather | solution.py:116
  38.5 15.1 %collective-permute-start = (bf16[64,1024]{1,0:T(8,128)(2,1)S(1)}, bf16[64,1024]{1,0:T(8,128)(2,1)S(1)}, u32[]{:S(2)}, u32[]{:S(2)}) collective-permute-start(bf16[64,1024]{1,0:T(8,128)(2,1)S(1)} %copy.49), channel_id=1, source_target_pairs={{0,1},{1,4},{4,5},{5,8},{8,9},{9,12},{12,13},{2,3},{3,6},{6,7},{7,... | collective-permute-start | bytes 393224 | tf_op jit(solution)/shard_map/ppermute | solution.py:21
  41.7 12.0 %collective-permute-start.1 = (bf16[64,1024]{1,0:T(8,128)(2,1)}, bf16[64,1024]{1,0:T(8,128)(2,1)S(1)}, u32[]{:S(2)}, u32[]{:S(2)}) collective-permute-start(bf16[64,1024]{1,0:T(8,128)(2,1)} %copy.51), channel_id=1, source_target_pairs={{1,0},{4,1},{5,4},{8,5},{9,8},{12,9},{13,12},{3,2},{6,3},{7,6},{10... | collective-permute-start | bytes 393224 | tf_op jit(solution)/shard_map/ppermute | solution.py:23
  51.0 2.7 %copy-start.4 = (bf16[1024,1024]{1,0:T(8,128)(2,1)S(1)}, bf16[1024,1024]{1,0:T(8,128)(2,1)}, u32[]{:S(2)}) copy-start(bf16[1024,1024]{1,0:T(8,128)(2,1)} %copy.50) | copy-start | bytes 6291460
  53.4 14.7 %copy-start.10 = (bf16[8,128,8,64]{1,3,2,0:T(8,128)(2,1)}, bf16[8,128,8,64]{1,3,2,0:T(8,128)(2,1)S(1)}, u32[]{:S(2)}) copy-start(bf16[8,128,8,64]{1,3,2,0:T(8,128)(2,1)S(1)} %copy.56) | copy-start | bytes 3145732
  57.6 4.3 %copy-start.5 = (bf16[128,8,8,128]{3,1,2,0:T(8,128)(2,1)S(1)}, bf16[128,8,8,128]{3,1,2,0:T(8,128)(2,1)}, u32[]{:S(2)}) copy-start(bf16[128,8,8,128]{3,1,2,0:T(8,128)(2,1)} %get-tuple-element.11) | copy-start | bytes 6291460
  63.8 4.3 %copy-start.7 = (bf16[8,128,8,128]{1,3,2,0:T(8,128)(2,1)S(1)}, bf16[8,128,8,128]{1,3,2,0:T(8,128)(2,1)}, u32[]{:S(2)}) copy-start(bf16[8,128,8,128]{1,3,2,0:T(8,128)(2,1)} %copy.53) | copy-start | bytes 6291460
  89.0 2.5 %copy-start.11 = (bf16[8,128,8,64]{1,3,2,0:T(8,128)(2,1)S(1)}, bf16[8,128,8,64]{1,3,2,0:T(8,128)(2,1)}, u32[]{:S(2)}) copy-start(bf16[8,128,8,64]{1,3,2,0:T(8,128)(2,1)} %copy-done.10) | copy-start | bytes 3145732
  91.5 9.2 %slice-start = ((s8[8388608]{0:T(1024)(128)(4,1)}), s8[4194304]{0:T(1024)(128)(4,1)S(1)}, s32[]{:S(2)}) async-start(s8[8388608]{0:T(1024)(128)(4,1)} %bitcast.85), calls=%async_computation.4 | async-start | bytes 8388608
  95.5 5.2 %copy-start.8 = (bf16[8,128,8,128]{1,3,2,0:T(8,128)(2,1)S(1)}, bf16[8,128,8,128]{1,3,2,0:T(8,128)(2,1)}, u32[]{:S(2)}) copy-start(bf16[8,128,8,128]{1,3,2,0:T(8,128)(2,1)} %copy.53) | copy-start | bytes 6291460
  95.5 5.2 %copy-start.9 = (bf16[8,128,8,128]{1,3,2,0:T(8,128)(2,1)S(1)}, bf16[8,128,8,128]{1,3,2,0:T(8,128)(2,1)}, u32[]{:S(2)}) copy-start(bf16[8,128,8,128]{1,3,2,0:T(8,128)(2,1)} %copy.54) | copy-start | bytes 6291460
  95.5 5.2 %slice-start.1 = ((s8[8388608]{0:T(1024)(128)(4,1)}), s8[4194304]{0:T(1024)(128)(4,1)S(1)}, s32[]{:S(2)}) async-start(s8[8388608]{0:T(1024)(128)(4,1)} %bitcast.85), calls=%async_computation.5 | async-start | bytes 8388608
  105.4 33.3 %copy-start.18 = (bf16[1024,512]{1,0:T(8,128)(2,1)S(1)}, bf16[1024,512]{1,0:T(8,128)(2,1)}, u32[]{:S(2)}) copy-start(bf16[1024,512]{1,0:T(8,128)(2,1)} %param.16) | copy-start | bytes 3145732
  106.7 66.2 %reduce-scatter.2.cloned.1.call-start = ((), (), s32[]{:S(2)}) async-start(), calls=%async_computation.2 | async-start | bytes 73728 | tf_op jit(solution)/shard_map/reduce_scatter | solution.py:130
  138.7 35.6 %copy-start.1 = (bf16[1024,512]{1,0:T(8,128)(2,1)S(1)}, bf16[1024,512]{1,0:T(8,128)(2,1)}, u32[]{:S(2)}) copy-start(bf16[1024,512]{1,0:T(8,128)(2,1)} %param.13) | copy-start | bytes 3145732
  141.6 32.6 %copy-start.12 = (bf16[1024,512]{1,0:T(8,128)(2,1)}, bf16[1024,512]{1,0:T(8,128)(2,1)S(1)}, u32[]{:S(2)}) copy-start(bf16[1024,512]{1,0:T(8,128)(2,1)S(1)} %convolution_convert_fusion) | copy-start | bytes 3145732
  (2 other events, 2.9 us)
Sparse Core Ops, SparseCore 0:
  34.7 51.1 all-gather.5
  106.8 31.8 all-gather.3
  142.8 30.0 reduce-scatter.1
